TPU v7x, 32 devices: a whole 2x2x4 slice. The times are simulated.
32 devices in a mesh: rcv: 4 (over y, core), slab: 8 (over z, x).
Axes of the slice: x: 2, y: 2, z: 4, core: 2. Of those that a mesh axis runs over, the one named last changes fastest.
Arguments:
- displacement: bfloat16 [2, 16, 3, 16, 16, 1024], P(None, None, None, 'slab'), may hold values from -6 to 6
- green: bfloat16 [8, 16, 6, 16, 16, 1024], P('rcv', None, None, 'slab'), may hold values from -0.1796875 to 0.1796875
- lame_lambda: float32 [16, 16, 1024], P('slab'), may hold values from 0.5 to 2
- shear_modulus: float32 [16, 16, 1024], P('slab'), may hold values from 0.3 to 1.5
- filters: float32 [2, 8, 9], P(None, 'rcv'), may hold values from -2 to 2
- pairs: int32 [2, 8], P(None, 'rcv'), may hold values 0 or 1
Outputs:
- kernels: float32 [2, 16, 16, 1024], P(None, 'slab', 'rcv')
Inputs may be any that keep to these rules, and one draw needn't show every extreme that they name: `pairs`: 1 marks a pair that is used, 0 one that is not.
All inputs are finite; a program needn't handle non-finite values. No bound on the sum of `pairs` on one device may be relied on, other than what follows from the above.
Results may differ from a plain program's by a relative error of at most 0.0029.
Values may be sent and summed in bfloat16 or wider, within the bound.
No kernel may reach another device: no remote copies, remote signals or barrier semaphores. Data moves between devices by JAX's collectives and lax.ppermute only.
A program may use at most 192 MiB of HBM per device.

v0:
```python
import functools
import jax
import jax.numpy as jnp
import numpy as np
from jax import lax
from jax.experimental import pallas as pl
from jax.experimental.pallas import tpu as pltpu
from jax.sharding import PartitionSpec as P

LANES = 128
F32 = jnp.float32
BF16 = jnp.bfloat16
ANY = pl.BlockSpec(memory_space=pl.ANY)
SMEM = pl.BlockSpec(memory_space=pltpu.SMEM)
VMEM = pl.BlockSpec(memory_space=pltpu.VMEM)


def stencil(offset):
    return 8.0 * (offset == 1) - 8.0 * (offset == -1) - 1.0 * (offset == 2) + 1.0 * (offset == -2)


def stencils(snaps, rows, width):
    place = np.arange(width)
    dcol = stencil(place[:, None] - place[None, :])
    snap = np.arange(snaps)
    same = snap[:, None] == snap[None, :]
    drow = []
    for h in range(2):
        row = np.arange(rows // 2) + h * (rows // 2)
        band = stencil(np.arange(rows)[None, :] - row[:, None])
        drow.append(np.kron(same, band))
    return jnp.asarray(dcol, BF16), jnp.asarray(np.stack(drow), BF16)


def iota(shape, axis):
    return lax.broadcasted_iota(jnp.int32, shape, axis)


def in_vmem(x):
    return pltpu.with_memory_space_constraint(x, pltpu.VMEM)


def in_hbm(x):
    return pltpu.with_memory_space_constraint(x, pltpu.HBM)


def two_parts(high, low):
    return high.astype(F32) + low.astype(F32)


def over(x, n):
    if n & (n - 1):
        return lax.div(x, jnp.int32(n)), lax.rem(x, jnp.int32(n))
    return lax.shift_right_logical(x, jnp.int32(n.bit_length() - 1)), x & jnp.int32(n - 1)


def fill_mix(filters_ref, pairs_ref, mix_ref, half):
    sources, stations, lags = filters_ref.shape
    points = mix_ref.shape[0] // sources
    snaps = points // half
    depth = mix_ref.shape[1]
    side = depth // 2
    shape = (snaps, stations * snaps)
    station, at = over(iota(shape, 1), snaps)
    lag = iota(shape, 0) - at + lags // 2
    same = over(iota((points, side), 0), half)[1] == over(iota((points, side), 1), half)[1]
    fans = [(over(iota((side, side), 1) + k * side, half)[0] == iota((side, side), 0)).astype(BF16) for k in range(2)]

    def spread(*accs):
        for unit in range(2):
            pltpu.matmul_push_rhs(fans[unit], staging_register=0, mxu_index=unit)
        for e in range(sources):
            table = jnp.zeros(shape, F32)
            for r in range(stations):
                used = pairs_ref[e, r].astype(F32)
                for j in range(lags):
                    table = jnp.where((station == r) & (lag == j), used * filters_ref[e, r, j], table)
            high = table.astype(BF16).astype(F32)
            taps = jnp.concatenate([high, table - high], axis=1)
            tall = jnp.broadcast_to(taps[:, None, :], (snaps, half, taps.shape[1])).reshape(points, taps.shape[1])
            lhs = jnp.concatenate([tall, jnp.zeros((points, side - taps.shape[1]), F32)], axis=1).astype(BF16)
            for unit in range(2):
                pltpu.matmul_acc_lhs(accs[unit], lhs, load_staged_rhs=0 if e == 0 else None)
                full = pltpu.matmul_pop(accs[unit])
                mix_ref[pl.ds(e * points, points), pl.ds(unit * side, side)] = jnp.where(same, full, 0.0).astype(BF16)

    pl.run_scoped(spread, *[pltpu.ACC(unit)((points, side), F32) for unit in range(2)])


def own_columns(displacement, me, slab, width, sizes):
    _, snaps, comps, planes, rows, _ = displacement.shape
    pieces = len(sizes)
    marks = [divmod(sum(sizes[:k]), snaps) for k in range(pieces)]

    def kernel(me_ref, slab_ref, src, *rest):
        outs, sems = rest[:-1], rest[-1]
        here = pl.ds(pl.multiple_of(me_ref[0] * width, width), width)
        copies = [
            pltpu.make_async_copy(src.at[e, pl.ds(s, size), :, :, :, here], outs[k], sems.at[k])
            for k, ((e, s), size) in enumerate(zip(marks, sizes))
        ]
        for copy in copies:
            copy.start()
        for copy in copies:
            copy.wait()

    return pl.pallas_call(
        kernel,
        out_shape=[jax.ShapeDtypeStruct((size, comps, planes, rows, width), displacement.dtype) for size in sizes],
        in_specs=[SMEM] * 2 + [ANY],
        out_specs=[VMEM] * pieces,
        scratch_shapes=[pltpu.SemaphoreType.DMA((pieces,))],
        compiler_params=pltpu.CompilerParams(vmem_limit_bytes=8 * 2**20),
        name="own_columns",
    )(me, slab, in_hbm(displacement))


def local_body(me, bits, first, tables, green_ref, added, z_ref, gs, xs, ys):
    mix_ref, dcol_ref, drow_ref, u_ref, lam_ref, mu_ref = tables
    count, _, planes, rows, width = z_ref.shape
    stations, snaps = green_ref.shape[:2]
    cols = u_ref.shape[-1]
    half = rows // 2
    points = snaps * half
    block = me ^ bits
    inside_half = pl.ds(pl.multiple_of((block & 1) * width, width), width)
    here = pl.ds(pl.multiple_of(block * width, width), width)
    before = pl.ds(pl.multiple_of(jnp.maximum(block * width - LANES, 0), LANES), LANES)
    behind = pl.ds(pl.multiple_of(jnp.minimum(block * width + width, cols - LANES), LANES), LANES)
    span = lambda h: pl.ds(h * half, half)
    space = lambda unit, size: pltpu.ACC(unit)((size, width), F32)

    lane = iota((half, LANES), 1)
    inner_left = jnp.where(block == 0, 0.0, 1.0)
    inner_right = jnp.where(block == cols // width - 1, 0.0, 1.0)
    left_2 = jnp.where(lane < 2, 1.0, 0.0) * inner_left
    left_1 = jnp.where(lane == 0, -8.0, 0.0) * inner_left
    right_2 = jnp.where(lane >= LANES - 2, -1.0, 0.0) * inner_right
    right_1 = jnp.where(lane == LANES - 1, 8.0, 0.0) * inner_right

    def one(index, carry):
        now, e = over(index, count)
        quake = first + e

        def filtered(h):
            def run(*accs):
                for k in range(3):
                    for unit in range(2):
                        tile = green_ref[:, :, 2 * k + unit, now, span(h), inside_half].reshape(stations * points, width)
                        pltpu.matmul_push_rhs(tile, staging_register=k % 2, mxu_index=unit)
                    for part in range(2):
                        row = pl.ds(pl.multiple_of(quake * points, points), points)
                        lhs = mix_ref[row, pl.ds(part * stations * points, stations * points)]
                        for unit in range(2):
                            acc = accs[2 * unit + k % 2]
                            pltpu.matmul_acc_lhs(acc, lhs, load_staged_rhs=k % 2 if part == 0 else None)
                    for unit in range(2):
                        gs[2 * k + unit, h] = pltpu.matmul_pop(accs[2 * unit + k % 2])

            pl.run_scoped(run, *[space(unit, points) for unit in range(2) for _ in range(2)])

        whole = [u_ref[quake, :, i, now, :, here].reshape(2 * points, width) for i in range(3)]

        def columns(*accs):
            for unit in range(2):
                pltpu.matmul_push_rhs(dcol_ref[...], staging_register=0, mxu_index=unit)
            for unit in range(2):
                pltpu.matmul_acc_lhs(accs[2 * unit], whole[unit], load_staged_rhs=0)
                pltpu.matmul_acc_lhs(accs[2 * unit + 1], whole[2][unit * points : (unit + 1) * points])
            for unit in range(2):
                xs[unit] = pltpu.matmul_pop(accs[2 * unit])
                xs[2, pl.ds(unit * points, points)] = pltpu.matmul_pop(accs[2 * unit + 1])

        def lines(*accs):
            for unit in range(2):
                pltpu.matmul_push_rhs(whole[unit], staging_register=0, mxu_index=unit)
                pltpu.matmul_push_rhs(whole[2], staging_register=1, mxu_index=unit)
            for unit in range(2):
                pltpu.matmul_acc_lhs(accs[3 * unit], drow_ref[0], load_staged_rhs=0)
                pltpu.matmul_acc_lhs(accs[3 * unit + 1], drow_ref[1])
                pltpu.matmul_acc_lhs(accs[3 * unit + 2], drow_ref[unit], load_staged_rhs=1)
            for unit in range(2):
                ys[unit, 0] = pltpu.matmul_pop(accs[3 * unit])
                ys[unit, 1] = pltpu.matmul_pop(accs[3 * unit + 1])
                ys[2, unit] = pltpu.matmul_pop(accs[3 * unit + 2])

        def along_columns(i, s, h):
            left = u_ref[quake, s, i, now, span(h), before].astype(F32)
            right = u_ref[quake, s, i, now, span(h), behind].astype(F32)
            left = pltpu.roll(left, 2, 1) * left_2 + pltpu.roll(left, 1, 1) * left_1
            right = pltpu.roll(right, LANES - 2, 1) * right_2 + pltpu.roll(right, LANES - 1, 1) * right_1
            inside = xs[i, pl.ds((2 * s + h) * half, half)]
            middle = inside[:, LANES : width - LANES]
            parts = [inside[:, :LANES] + left] + ([middle] if middle.shape[1] else [])
            return jnp.concatenate(parts + [inside[:, width - LANES :] + right], axis=1)

        def combine(h):
            vol = dev = jnp.zeros((half, width), F32)
            lam = lam_ref[now, span(h), here]
            mu2 = 2.0 * mu_ref[now, span(h), here]
            for s in range(snaps):
                at = pl.ds(s * half, half)
                xs0, xs1, xs2 = (along_columns(i, s, h) for i in range(3))
                gxx, gyy, gzz, gyz, gxz, gxy = (gs[c, h, at] for c in range(6))
                gtr = gxx + gyy + gzz
                dxx, dyy = xs0, ys[1, h, at]
                vol = vol + (dxx + dyy) * gtr
                dev = dev + (dxx * gxx + dyy * gyy) + (ys[2, h, at] * gyz + xs2 * gxz)
                dev = dev + (xs1 + ys[0, h, at]) * gxy
                for i, z in enumerate((mu2 * gxz, mu2 * gyz, lam * gtr + mu2 * gzz)):
                    for ref in added:
                        z = z + ref[e, i * snaps + s, now, span(h)].astype(F32)
                    z_ref[e, i * snaps + s, now, span(h)] = z.astype(BF16)
            part = (lam * vol + mu2 * dev) / 12.0
            for ref in added:
                part = part + two_parts(ref[e, 3 * snaps, now, span(h)], ref[e, 3 * snaps + 1, now, span(h)])
            high = part.astype(BF16)
            z_ref[e, 3 * snaps, now, span(h)] = high
            z_ref[e, 3 * snaps + 1, now, span(h)] = (part - high.astype(F32)).astype(BF16)

        pl.run_scoped(columns, *[space(unit, size) for unit in range(2) for size in (2 * points, points)])
        pl.run_scoped(lines, *[space(unit, points) for unit in range(2) for _ in range(3)])
        filtered(0)
        filtered(1)
        combine(0)
        combine(1)
        return carry

    lax.fori_loop(0, planes * count, one, 0)


def half_columns(ref, half, width):
    return ref.at[..., pl.ds(pl.multiple_of(half * 2 * width, 2 * width), 2 * width)]


def first_kernel(me_ref, filters_ref, pairs_ref, u_src, green_src, *rest, bits, waits):
    (lam_src, mu_src, dcol_src, drow_src), rest = rest[:4], rest[4 + waits :]
    z_ref, green_ref, mix_ref, dcol_ref, drow_ref, u_ref, lam_ref, mu_ref, gs, xs, ys, sems = rest
    rows, width = z_ref.shape[-2:]
    me = me_ref[0]
    block = me ^ bits

    def green_block(block, sem):
        there = pl.ds(pl.multiple_of(block * width, width), width)
        inside = pl.ds(pl.multiple_of((block & 1) * width, width), width)
        return pltpu.make_async_copy(green_src.at[..., there], green_ref.at[..., inside], sem)

    early = [pltpu.make_async_copy(u_src.at[0], u_ref.at[0], sems.at[6]), green_block(block, sems.at[0])]
    smalls = ((lam_src, lam_ref), (mu_src, mu_ref), (dcol_src, dcol_ref), (drow_src, drow_ref))
    early += [pltpu.make_async_copy(src, ref, sems.at[1 + k]) for k, (src, ref) in enumerate(smalls)]
    late = [green_block(block ^ 1, sems.at[5])]
    for copy in early:
        copy.start()
    fill_mix(filters_ref, pairs_ref, mix_ref, rows // 2)
    for copy in early:
        copy.wait()
    for copy in late:
        copy.start()
    local_body(me, bits, 0, (mix_ref, dcol_ref, drow_ref, u_ref, lam_ref, mu_ref), green_ref, (), z_ref, gs, xs, ys)
    for copy in late:
        copy.wait()


def z_shape(count, displacement, width):
    snaps, planes, rows = displacement.shape[1], displacement.shape[3], displacement.shape[4]
    return jax.ShapeDtypeStruct((count, 3 * snaps + 2, planes, rows, width), BF16)


def local_scratch(displacement, width):
    points = displacement.shape[1] * displacement.shape[4]
    return [
        pltpu.VMEM((6, 2, points // 2, width), F32),
        pltpu.VMEM((3, points, width), F32),
        pltpu.VMEM((3, 2, points // 2, width), F32),
    ]


def local_cost(count, green, displacement, width):
    _, snaps, _, planes, rows, _ = displacement.shape
    stations = green.shape[0]
    points = snaps * rows
    return pl.CostEstimate(
        flops=int(count * planes * 2 * width * points * (6 * stations * points + 3 * width + 3 * points)),
        bytes_accessed=int(count * planes * width * rows * snaps * (6 * stations + 9) * 2),
        transcendentals=0,
    )


def first_terms(me, bits, filters, pairs, displacement, green, lam, mu, width, after):
    sources, snaps, _, planes, rows, _ = displacement.shape
    stations = green.shape[0]
    fixed = stencils(snaps, rows, width)
    kept = [((stations, snaps, 6, planes, rows, 2 * width), green.dtype)]
    points = snaps * rows // 2
    kept.append(((sources * points, 2 * stations * points), BF16))
    kept += [(array.shape, array.dtype) for array in fixed + (displacement, lam, mu)]
    z, near, *tables = pl.pallas_call(
        functools.partial(first_kernel, bits=bits, waits=len(after)),
        out_shape=[z_shape(1, displacement, width)] + [pltpu.VMEM(*one) for one in kept],
        in_specs=[SMEM] * 3 + [ANY] * (6 + len(after)),
        out_specs=[VMEM] * (1 + len(kept)),
        scratch_shapes=local_scratch(displacement, width) + [pltpu.SemaphoreType.DMA((7,))],
        cost_estimate=local_cost(1, green, displacement, width),
        compiler_params=pltpu.CompilerParams(vmem_limit_bytes=16 * 2**20),
        name="first_terms",
    )(me, *map(in_hbm, (filters, pairs, displacement, green, lam, mu) + fixed), *after)
    return z, near, tuple(tables)


def local_kernel(me_ref, *refs, bits, first, waits, more, fetch, fill):
    me = me_ref[0]
    tables, green_ref, rest = refs[:6], refs[6], refs[7:]
    if fetch or fill:
        source, rest = rest[0], rest[1:]
    rest = rest[waits:]
    added, rest = rest[:more], rest[more:]
    if fetch:
        z_ref, other_ref, gs, xs, ys, sem = rest
        half = lax.shift_right_logical(me, 1)
        copy = pltpu.make_async_copy(half_columns(source, half, z_ref.shape[-1]), other_ref, sem)
        copy.start()
    elif fill:
        z_ref, u_ref, gs, xs, ys, sem = rest
        others = pl.ds(1, u_ref.shape[0] - 1)
        copy = pltpu.make_async_copy(source.at[others], u_ref.at[others], sem)
        copy.start()
    else:
        z_ref, gs, xs, ys = rest
    local_body(me, bits, first, tables, green_ref, added, z_ref, gs, xs, ys)
    if fetch or fill:
        copy.wait()


def local_terms(me, bits, first, count, tables, green_half, green, displacement, width, after=(), add=(), fetch=False, fill=False):
    out_shape = [z_shape(count, displacement, width)]
    scratch = local_scratch(displacement, width)
    if fetch:
        out_shape.append(pltpu.VMEM(green_half.shape, green_half.dtype))
        scratch.append(pltpu.SemaphoreType.DMA(()))
    if fill:
        out_shape.append(pltpu.VMEM(displacement.shape, displacement.dtype))
        scratch.append(pltpu.SemaphoreType.DMA(()))
    return pl.pallas_call(
        functools.partial(local_kernel, bits=bits, first=first, waits=len(after), more=len(add), fetch=fetch, fill=fill),
        out_shape=out_shape,
        in_specs=[SMEM] + [VMEM] * 7 + [ANY] * (fetch + fill + len(after)) + [VMEM] * len(add),
        out_specs=[VMEM] * len(out_shape),
        scratch_shapes=scratch,
        input_output_aliases={4: 1} if fill else {},
        cost_estimate=local_cost(count, green, displacement, width),
        compiler_params=pltpu.CompilerParams(vmem_limit_bytes=16 * 2**20),
        name="local_terms",
    )(me, *tables, green_half, *([in_hbm(green)] if fetch else [in_hbm(displacement)] if fill else []), *after, *map(in_vmem, add))


def depth_kernel(me_ref, slab_ref, *refs, groups, slabs, lasts):
    pieces, rest = refs[:lasts[0]], refs[lasts[0] :]
    z0_ref, z1_ref, outs = rest[0], rest[1], rest[2:]
    _, rows, width = z1_ref.shape[2:]
    source = lasts[1]
    snaps = (z1_ref.shape[1] - 2) // 3
    slab = slab_ref[0]
    even = slab % 2 == 0
    known = jnp.where(even, slab > 0, slab < slabs - 1).astype(F32)
    pick = lambda one, other: jnp.where(even, jnp.float32(one), jnp.float32(other))
    coefs = [pick(*both) for both in ((-1, 1), (0, -8), (1, -1), (-8, 0), (8, 0), (-1, 1), (0, 8), (1, -1))]
    coefs = [coef * known if k % 4 >= 2 else coef for k, coef in enumerate(coefs)]
    total = [
        sum(two_parts(ref[k, 3 * snaps, p], ref[k, 3 * snaps + 1, p]) for ref, k in ((z0_ref, source), (z1_ref, 0)))
        for p in range(2)
    ]
    carry = tuple(jnp.zeros((rows, width), F32) for _ in range(2))
    at = 0
    for own_ref, near_ref, far_ref in zip(pieces[0::3], pieces[1::3], pieces[2::3]):

        def step(s, carry, at=at, own_ref=own_ref, near_ref=near_ref, far_ref=far_ref):
            top, bottom = carry
            for i in range(3):
                own0, own1 = own_ref[s, i, 0].astype(F32), own_ref[s, i, 1].astype(F32)
                n0, n1 = near_ref[s, i, 0].astype(F32), near_ref[s, i, 1].astype(F32)
                f0, f1 = far_ref[s, i, 0].astype(F32), far_ref[s, i, 1].astype(F32)
                d0 = 8.0 * own1 + (coefs[0] * n0 + coefs[1] * n1) + (coefs[2] * f0 + coefs[3] * f1)
                d1 = (coefs[4] * n0 + coefs[5] * n1) + (coefs[6] * f0 + coefs[7] * f1) - 8.0 * own0
                k = i * snaps + at + s
                z = [z0_ref[source, k, p].astype(F32) + z1_ref[0, k, p].astype(F32) for p in range(2)]
                top = top + z[0] * d0
                bottom = bottom + z[1] * d1
            return top, bottom

        count = own_ref.shape[0]
        carry = lax.fori_loop(0, count, step, carry, unroll=2)
        at += count
    part = rows // groups
    held = outs[-1]
    for p in range(2):
        value = total[p] + carry[p] / 12.0
        for q in range(groups):
            held[q, p] = value[q * part : (q + 1) * part]
    for bits, out in enumerate(outs[:-1]):
        out[...] = held[me_ref[0] ^ bits]


def depth_terms(me, slab, pieces, z0, z1, source, groups, slabs):
    planes, rows, width = z1.shape[2:]
    shape = (planes, rows // groups, width)
    flat = [array for piece in pieces for array in piece]
    return pl.pallas_call(
        functools.partial(depth_kernel, groups=groups, slabs=slabs, lasts=(len(flat), source)),
        out_shape=[jax.ShapeDtypeStruct(shape, F32)] * groups,
        in_specs=[SMEM, SMEM] + [VMEM] * (len(flat) + 2),
        out_specs=[VMEM] * groups,
        scratch_shapes=[pltpu.VMEM((groups,) + shape, F32)],
        compiler_params=pltpu.CompilerParams(vmem_limit_bytes=8 * 2**20),
        name="depth_terms",
    )(me, slab, *map(in_vmem, flat + [z0, z1]))


def join_kernel(me_ref, *refs):
    pieces, out = refs[:-1], refs[-1]
    sources = out.shape[0]
    width = pieces[0].shape[-1]
    for k, piece in enumerate(pieces):
        bits, e = divmod(k, sources)
        out[e, :, :, pl.ds(pl.multiple_of((me_ref[0] ^ bits) * width, width), width)] = piece[...]


def join_columns(me, pieces, sources):
    planes, part, width = pieces[0].shape
    return pl.pallas_call(
        join_kernel,
        out_shape=jax.ShapeDtypeStruct((sources, planes, part, width * len(pieces) // sources), F32),
        in_specs=[SMEM] + [VMEM] * len(pieces),
        out_specs=VMEM,
        compiler_params=pltpu.CompilerParams(vmem_limit_bytes=8 * 2**20),
        name="join_columns",
    )(me, *map(in_vmem, pieces))


SHARES = (4, 4, 5, 3)


def on_device(displacement, green, lame_lambda, shear_modulus, filters, pairs):
    sources, snaps, _, _, _, cols = displacement.shape
    groups = lax.axis_size("rcv")
    slabs = lax.axis_size("slab")
    me = lax.axis_index("rcv").reshape(1)
    slab = lax.axis_index("slab").reshape(1)
    width = cols // groups
    pair_swap = [(i, i ^ 1) for i in range(slabs)]
    back = [(i, i - 2 if i % 2 == 0 else i + 2) for i in range(slabs)]
    back = [(i, j) for i, j in back if 0 <= j < slabs]
    chain = [(i, i + 2 if i % 2 == 0 else i - 2) for i in range(slabs)]
    chain = [(i, j) for i, j in chain if 0 <= j < slabs]
    onward = [(i, (i + 2 if i % 2 == 0 else i - 2) % slabs) for i in range(slabs)]

    def swap(x, bit):
        return lax.ppermute(x, "rcv", [(i, i ^ bit) for i in range(groups)])

    def along(x, links):
        return lax.ppermute(x, "slab", links)

    def terms(bits, first, count, half, after=(), add=(), **extra):
        return local_terms(me, bits, first, count, tables, half, green, displacement, width, after, add, **extra)

    total_snaps = sources * snaps
    unit = total_snaps // sum(SHARES)
    sizes = [share * unit for share in SHARES]
    own = own_columns(displacement, me, slab, width, sizes)
    near = [along(piece, pair_swap) for piece in own]
    far = [along(piece, onward if k < len(near) - 2 else chain) for k, piece in enumerate(near[:-1])]
    last = len(own) - 1
    far.append(along(along(own[last], back), pair_swap))

    across = []
    for e in range(sources):
        if e == 0:
            last, far_half, tables = first_terms(
                me, 3, filters, pairs, displacement, green, lame_lambda, shear_modulus, width, (own[0],)
            )
        else:
            last, near_half = terms(3, e, 1, far_half, (last,), fetch=True)
        sent = swap(last, 1)
        last, *filled = terms(2, e, 1, far_half, (last,), (sent,), fill=e == 0)
        if filled:
            tables = tables[:3] + tuple(filled) + tables[4:]
        across.append(swap(last, 2))
    (last,) = terms(1, 0, sources, near_half, (last,))
    (z0,) = terms(0, 0, sources, near_half, (last,), (swap(last, 1),))

    pieces = []
    for e in range(sources):
        mine = [k for k in range(len(SHARES)) if sum(sizes[:k]) // snaps == e]
        pieces.append(depth_terms(me, slab, [(own[k], near[k], far[k]) for k in mine], z0, across[e], e, groups, slabs))
    ends = []
    for bits in range(groups):
        for e in range(sources):
            piece = pieces[e][bits]
            ends.append(swap(piece, bits) if bits else piece)
    return join_columns(me, ends, sources)


def solution(mesh):
    placed = (
        P(None, None, None, "slab", None, None),
        P("rcv", None, None, "slab", None, None),
        P("slab", None, None),
        P("slab", None, None),
        P(None, "rcv", None),
        P(None, "rcv"),
    )
    return jax.shard_map(
        on_device,
        mesh=mesh,
        in_specs=placed,
        out_specs=P(None, "slab", "rcv", None),
        check_vma=False,
    )
```

profile of v0, /device:TPU:0, one launch (start us, length us, event | category | flops | bytes accessed | tf_op | source)
XLA Modules:
  0.0 102.4 jit_solution(7751919221754671969)
XLA Ops:
  0.0 1.4 %own_columns.1 = (bf16[8,3,2,16,256]{4,3,2,1,0:T(8,128)(2,1)S(1)}, bf16[8,3,2,16,256]{4,3,2,1,0:T(8,128)(2,1)S(1)}, bf16[10,3,2,16,256]{4,3,2,1,0:T(8,128)(2,1)S(1)}, bf16[6,3,2,16,256]{4,3,2,1,0:T(8,128)(2,1)S(1)}) custom-call(s32[1]{0:T(128)} %bitcast.me_ref, s32[1]{0:T(128)} %bitcast.1.slab_ref, bf16[2,16,3,2,16,1024]{5,4,3,2,1,0:T(8,128)(2,1)} %refs_7_.2), custom_call_target="tpu_custom_call" | custom-call | tf_op jit(solution)/shard_map/own_columns/pallas_call | solution.py:107
  1.4 5.9 %first_terms.1 = (bf16[1,50,2,16,256]{4,3,2,1,0:T(8,128)(2,1)S(1)}, bf16[2,16,6,2,16,512]{5,4,3,2,1,0:T(8,128)(2,1)S(1)}, bf16[256,512]{1,0:T(8,128)(2,1)S(1)}, ...) custom-call(s32[1]{0:T(128)} %bitcast.me_ref, ...), custom_call_target="tpu_custom_call" | custom-call | flops 1207959552 | bytes 5505024 | tf_op jit(solution)/shard_map/first_terms/pallas_call | solution.py:297
  7.3 0.5 collective-permute-start.4
  7.9 2.0 %collective-permute-done.4.refs_9_ = bf16[1,50,2,16,256]{4,3,2,1,0:T(8,128)(2,1)S(1)} collective-permute-done((bf16[1,50,2,16,256]{4,3,2,1,0:T(8,128)(2,1)S(1)}, bf16[1,50,2,16,256]{4,3,2,1,0:T(8,128)(2,1)S(1)}, u32[]{:S(2)}, u32[]{:S(2)}) %collective-permute-start.4) | collective-permute-done | bytes 819232 | tf_op jit(solution)/shard_map/ppermute | solution.py:457
  9.8 2.3 %local_terms.5 = (bf16[1,50,2,16,256]{4,3,2,1,0:T(8,128)(2,1)S(1)}, bf16[2,16,3,2,16,1024]{5,4,3,2,1,0:T(8,128)(2,1)S(1)}) custom-call(s32[1]{0:T(128)} %bitcast.me_ref, bf16[256,512]{1,0:T(8,128)(2,1)S(1)} %get-tuple-element.31.refs_0_, bf16[256,256]{1,0:T(8,128)(2,1)S(1)} %get-tuple-element.32.refs_1_, ...), custom_call_target="tpu_custom_call", output_to_operand_aliasing={{1}: (4, {})} | custom-call | flops 1207959552 | bytes 5505024 | tf_op jit(solution)/shard_map/local_terms/pallas_call | solution.py:343
  12.2 2.8 %local_terms.6 = (bf16[1,50,2,16,256]{4,3,2,1,0:T(8,128)(2,1)S(1)}, bf16[2,16,6,2,16,512]{5,4,3,2,1,0:T(8,128)(2,1)S(1)}) custom-call(s32[1]{0:T(128)} %bitcast.me_ref, bf16[256,512]{1,0:T(8,128)(2,1)S(1)} %get-tuple-element.31.refs_0_, bf16[256,256]{1,0:T(8,128)(2,1)S(1)} %get-tuple-element.32.refs_1_, bf16[2,128,256]{2,1,0:T(8,128)(2,1)S(1)} %get-tuple-element.33.refs_2_, ...), custom_call_target="tpu_custom_call" | custom-call | flops 1207959552 | bytes 5505024 | tf_op jit(solution)/shard_map/local_terms/pallas_call | solution.py:343
  15.0 0.4 collective-permute-start.5
  15.4 2.0 %collective-permute-done.5.refs_8_ = bf16[1,50,2,16,256]{4,3,2,1,0:T(8,128)(2,1)S(1)} collective-permute-done((bf16[1,50,2,16,256]{4,3,2,1,0:T(8,128)(2,1)S(1)}, bf16[1,50,2,16,256]{4,3,2,1,0:T(8,128)(2,1)S(1)}, u32[]{:S(2)}, u32[]{:S(2)}) %collective-permute-start.5) | collective-permute-done | bytes 819232 | tf_op jit(solution)/shard_map/ppermute | solution.py:457
  17.4 2.3 %local_terms.7.refs_7_ = bf16[1,50,2,16,256]{4,3,2,1,0:T(8,128)(2,1)S(1)} custom-call(s32[1]{0:T(128)} %bitcast.me_ref, bf16[256,512]{1,0:T(8,128)(2,1)S(1)} %get-tuple-element.31.refs_0_, bf16[256,256]{1,0:T(8,128)(2,1)S(1)} %get-tuple-element.32.refs_1_, bf16[2,128,256]{2,1,0:T(8,128)(2,1)S(1)} %get-tuple-element.33.refs_2_, ...), custom_call_target="tpu_custom_call" | custom-call | flops 1207959552 | bytes 5505024 | tf_op jit(solution)/shard_map/local_terms/pallas_call | solution.py:343
  19.7 4.5 %local_terms.8.refs_7_ = bf16[2,50,2,16,256]{4,3,2,1,0:T(8,128)(2,1)S(1)} custom-call(s32[1]{0:T(128)} %bitcast.me_ref, bf16[256,512]{1,0:T(8,128)(2,1)S(1)} %get-tuple-element.31.refs_0_, bf16[256,256]{1,0:T(8,128)(2,1)S(1)} %get-tuple-element.32.refs_1_, bf16[2,128,256]{2,1,0:T(8,128)(2,1)S(1)} %get-tuple-element.33.refs_2_, ...), custom_call_target="tpu_custom_call" | custom-call | flops 2415919104 | bytes 11010048 | tf_op jit(solution)/shard_map/local_terms/pallas_call | solution.py:343
  24.2 0.4 collective-permute-start.6
  24.6 1.3 %collective-permute-start.11 = (bf16[6,3,2,16,256]{4,3,2,1,0:T(8,128)(2,1)S(1)}, bf16[6,3,2,16,256]{4,3,2,1,0:T(8,128)(2,1)S(1)}, u32[]{:S(2)}, u32[]{:S(2)}) collective-permute-start(bf16[6,3,2,16,256]{4,3,2,1,0:T(8,128)(2,1)S(1)} %get-tuple-element.45.refs_3_), channel_id=1, source_target_pairs={{1,3},{2,0},{3,5},{4,2},{5,7},{6,4},{9,11},{10,8},{11,13},{12,10},... | collective-permute-start | bytes 884744 | tf_op jit(solution)/shard_map/ppermute | solution.py:460
  25.9 4.9 %collective-permute-start = (bf16[8,3,2,16,256]{4,3,2,1,0:T(8,128)(2,1)S(1)}, bf16[8,3,2,16,256]{4,3,2,1,0:T(8,128)(2,1)S(1)}, u32[]{:S(2)}, u32[]{:S(2)}) collective-permute-start(bf16[8,3,2,16,256]{4,3,2,1,0:T(8,128)(2,1)S(1)} %get-tuple-element.29.rest_4_.refs_0_), channel_id=1, source_target_pairs={{0,1},{1,0},{2,3},{3,2},{4,5},{5,4},{6,7},{7,6},{8,9},{9,8},{10,11... | collective-permute-start | bytes 1179656 | tf_op jit(solution)/shard_map/ppermute | solution.py:460
  30.8 0.1 collective-permute-start.10
  30.9 1.9 %collective-permute-start.2 = (bf16[8,3,2,16,256]{4,3,2,1,0:T(8,128)(2,1)S(1)}, bf16[8,3,2,16,256]{4,3,2,1,0:T(8,128)(2,1)S(1)}, u32[]{:S(2)}, u32[]{:S(2)}) collective-permute-start(bf16[8,3,2,16,256]{4,3,2,1,0:T(8,128)(2,1)S(1)} %get-tuple-element.30.refs_3_), channel_id=1, source_target_pairs={{0,1},{1,0},{2,3},{3,2},{4,5},{5,4},{6,7},{7,6},{8,9},{9,8},{10,11... | collective-permute-start | bytes 1179656 | tf_op jit(solution)/shard_map/ppermute | solution.py:460
  32.8 4.0 %collective-permute-done.11 = bf16[6,3,2,16,256]{4,3,2,1,0:T(8,128)(2,1)S(1)} collective-permute-done((bf16[6,3,2,16,256]{4,3,2,1,0:T(8,128)(2,1)S(1)}, bf16[6,3,2,16,256]{4,3,2,1,0:T(8,128)(2,1)S(1)}, u32[]{:S(2)}, u32[]{:S(2)}) %collective-permute-start.11) | collective-permute-done | bytes 294944 | tf_op jit(solution)/shard_map/ppermute | solution.py:460
  36.8 0.8 collective-permute-start.8
  37.5 9.5 %collective-permute-done.10.refs_4_ = bf16[6,3,2,16,256]{4,3,2,1,0:T(8,128)(2,1)S(1)} collective-permute-done((bf16[6,3,2,16,256]{4,3,2,1,0:T(8,128)(2,1)S(1)}, bf16[6,3,2,16,256]{4,3,2,1,0:T(8,128)(2,1)S(1)}, u32[]{:S(2)}, u32[]{:S(2)}) %collective-permute-start.10) | collective-permute-done | bytes 294944 | tf_op jit(solution)/shard_map/ppermute | solution.py:460
  47.1 1.6 %collective-permute-start.13 = (bf16[1,50,2,16,256]{4,3,2,1,0:T(8,128)(2,1)S(1)}, bf16[1,50,2,16,256]{4,3,2,1,0:T(8,128)(2,1)S(1)}, u32[]{:S(2)}, u32[]{:S(2)}) collective-permute-start(bf16[1,50,2,16,256]{4,3,2,1,0:T(8,128)(2,1)S(1)} %local_terms.7.refs_7_), channel_id=1, source_target_pairs={{0,16},{8,24},{16,0},{24,8},{1,17},{9,25},{17,1},{25,9},{2,18},{10... | collective-permute-start | bytes 2457608 | tf_op jit(solution)/shard_map/ppermute | solution.py:457
  48.7 0.0 collective-permute-done.refs_1_
  48.7 0.5 collective-permute-start.7
  49.1 6.4 %collective-permute-done.2.refs_4_ = bf16[8,3,2,16,256]{4,3,2,1,0:T(8,128)(2,1)S(1)} collective-permute-done((bf16[8,3,2,16,256]{4,3,2,1,0:T(8,128)(2,1)S(1)}, bf16[8,3,2,16,256]{4,3,2,1,0:T(8,128)(2,1)S(1)}, u32[]{:S(2)}, u32[]{:S(2)}) %collective-permute-start.2) | collective-permute-done | bytes 393248 | tf_op jit(solution)/shard_map/ppermute | solution.py:460
  55.5 2.0 %collective-permute-start.12 = (bf16[6,3,2,16,256]{4,3,2,1,0:T(8,128)(2,1)S(1)}, bf16[6,3,2,16,256]{4,3,2,1,0:T(8,128)(2,1)S(1)}, u32[]{:S(2)}, u32[]{:S(2)}) collective-permute-start(bf16[6,3,2,16,256]{4,3,2,1,0:T(8,128)(2,1)S(1)} %collective-permute-done.11), channel_id=1, source_target_pairs={{0,1},{1,0},{2,3},{3,2},{4,5},{5,4},{6,7},{7,6},{8,9},{9,8},{10,11... | collective-permute-start | bytes 884744 | tf_op jit(solution)/shard_map/ppermute | solution.py:460
  57.5 8.5 %collective-permute-done.8.refs_1_ = bf16[10,3,2,16,256]{4,3,2,1,0:T(8,128)(2,1)S(1)} collective-permute-done((bf16[10,3,2,16,256]{4,3,2,1,0:T(8,128)(2,1)S(1)}, bf16[10,3,2,16,256]{4,3,2,1,0:T(8,128)(2,1)S(1)}, u32[]{:S(2)}, u32[]{:S(2)}) %collective-permute-start.8) | collective-permute-done | bytes 491552 | tf_op jit(solution)/shard_map/ppermute | solution.py:460
  66.0 3.5 %collective-permute-start.9 = (bf16[10,3,2,16,256]{4,3,2,1,0:T(8,128)(2,1)S(1)}, bf16[10,3,2,16,256]{4,3,2,1,0:T(8,128)(2,1)S(1)}, u32[]{:S(2)}, u32[]{:S(2)}) collective-permute-start(bf16[10,3,2,16,256]{4,3,2,1,0:T(8,128)(2,1)S(1)} %collective-permute-done.8.refs_1_), channel_id=1, source_target_pairs={{0,2},{2,4},{3,1},{4,6},{5,3},{7,5},{8,10},{10,12},{11,9},{12,14},... | collective-permute-start | bytes 1474568 | tf_op jit(solution)/shard_map/ppermute | solution.py:460
  69.6 2.2 %collective-permute-done.12.refs_5_ = bf16[6,3,2,16,256]{4,3,2,1,0:T(8,128)(2,1)S(1)} collective-permute-done((bf16[6,3,2,16,256]{4,3,2,1,0:T(8,128)(2,1)S(1)}, bf16[6,3,2,16,256]{4,3,2,1,0:T(8,128)(2,1)S(1)}, u32[]{:S(2)}, u32[]{:S(2)}) %collective-permute-start.12) | collective-permute-done | bytes 294944 | tf_op jit(solution)/shard_map/ppermute | solution.py:460
  71.8 1.6 %collective-permute-start.1 = (bf16[8,3,2,16,256]{4,3,2,1,0:T(8,128)(2,1)S(1)}, bf16[8,3,2,16,256]{4,3,2,1,0:T(8,128)(2,1)S(1)}, u32[]{:S(2)}, u32[]{:S(2)}) collective-permute-start(bf16[8,3,2,16,256]{4,3,2,1,0:T(8,128)(2,1)S(1)} %collective-permute-done.refs_1_), channel_id=1, source_target_pairs={{0,2},{1,7},{2,4},{3,1},{4,6},{5,3},{6,0},{7,5},{8,10},{9,15},{10,... | collective-permute-start | bytes 1179656 | tf_op jit(solution)/shard_map/ppermute | solution.py:460
  73.4 0.0 collective-permute-done.6.refs_8_
  73.4 1.6 %collective-permute-start.3 = (bf16[8,3,2,16,256]{4,3,2,1,0:T(8,128)(2,1)S(1)}, bf16[8,3,2,16,256]{4,3,2,1,0:T(8,128)(2,1)S(1)}, u32[]{:S(2)}, u32[]{:S(2)}) collective-permute-start(bf16[8,3,2,16,256]{4,3,2,1,0:T(8,128)(2,1)S(1)} %collective-permute-done.2.refs_4_), channel_id=1, source_target_pairs={{0,2},{1,7},{2,4},{3,1},{4,6},{5,3},{6,0},{7,5},{8,10},{9,15},{10,... | collective-permute-start | bytes 1179656 | tf_op jit(solution)/shard_map/ppermute | solution.py:460
  74.9 4.7 %local_terms.9.refs_6_ = bf16[2,50,2,16,256]{4,3,2,1,0:T(8,128)(2,1)S(1)} custom-call(s32[1]{0:T(128)} %bitcast.me_ref, bf16[256,512]{1,0:T(8,128)(2,1)S(1)} %get-tuple-element.31.refs_0_, bf16[256,256]{1,0:T(8,128)(2,1)S(1)} %get-tuple-element.32.refs_1_, bf16[2,128,256]{2,1,0:T(8,128)(2,1)S(1)} %get-tuple-element.33.refs_2_, ...), custom_call_target="tpu_custom_call" | custom-call | flops 2415919104 | bytes 11010048 | tf_op jit(solution)/shard_map/local_terms/pallas_call | solution.py:343
  79.7 1.5 %collective-permute-done.9.refs_2_ = bf16[10,3,2,16,256]{4,3,2,1,0:T(8,128)(2,1)S(1)} collective-permute-done((bf16[10,3,2,16,256]{4,3,2,1,0:T(8,128)(2,1)S(1)}, bf16[10,3,2,16,256]{4,3,2,1,0:T(8,128)(2,1)S(1)}, u32[]{:S(2)}, u32[]{:S(2)}) %collective-permute-start.9) | collective-permute-done | bytes 491552 | tf_op jit(solution)/shard_map/ppermute | solution.py:460
  81.1 0.0 collective-permute-done.13.refs_7_
  81.1 0.9 depth_terms.3
  82.1 0.1 collective-permute-start.15
  82.2 1.6 %collective-permute-start.17 = (f32[2,4,256]{2,1,0:T(4,128)S(1)}, f32[2,4,256]{2,1,0:T(4,128)S(1)}, u32[]{:S(2)}, u32[]{:S(2)}) collective-permute-start(f32[2,4,256]{2,1,0:T(4,128)S(1)} %get-tuple-element.50), channel_id=1, source_target_pairs={{0,16},{8,24},{16,0},{24,8},{1,17},{9,25},{17,1},{25,9},{2,18},{10... | collective-permute-start | bytes 24584 | tf_op jit(solution)/shard_map/ppermute | solution.py:457
  83.8 5.8 %collective-permute-done.1.refs_2_ = bf16[8,3,2,16,256]{4,3,2,1,0:T(8,128)(2,1)S(1)} collective-permute-done((bf16[8,3,2,16,256]{4,3,2,1,0:T(8,128)(2,1)S(1)}, bf16[8,3,2,16,256]{4,3,2,1,0:T(8,128)(2,1)S(1)}, u32[]{:S(2)}, u32[]{:S(2)}) %collective-permute-start.1) | collective-permute-done | bytes 393248 | tf_op jit(solution)/shard_map/ppermute | solution.py:460
  89.6 0.0 collective-permute-start.19
  89.6 6.4 %collective-permute-done.3.refs_5_ = bf16[8,3,2,16,256]{4,3,2,1,0:T(8,128)(2,1)S(1)} collective-permute-done((bf16[8,3,2,16,256]{4,3,2,1,0:T(8,128)(2,1)S(1)}, bf16[8,3,2,16,256]{4,3,2,1,0:T(8,128)(2,1)S(1)}, u32[]{:S(2)}, u32[]{:S(2)}) %collective-permute-start.3) | collective-permute-done | bytes 393248 | tf_op jit(solution)/shard_map/ppermute | solution.py:460
  95.9 0.0 collective-permute-done.7.refs_7_
  95.9 0.9 depth_terms.2
  96.9 0.1 collective-permute-start.14
  97.0 1.7 %collective-permute-start.16 = (f32[2,4,256]{2,1,0:T(4,128)S(1)}, f32[2,4,256]{2,1,0:T(4,128)S(1)}, u32[]{:S(2)}, u32[]{:S(2)}) collective-permute-start(f32[2,4,256]{2,1,0:T(4,128)S(1)} %get-tuple-element.49), channel_id=1, source_target_pairs={{0,16},{8,24},{16,0},{24,8},{1,17},{9,25},{17,1},{25,9},{2,18},{10... | collective-permute-start | bytes 24584 | tf_op jit(solution)/shard_map/ppermute | solution.py:457
  98.6 0.0 collective-permute-done.15.refs_3_
  98.6 0.2 collective-permute-start.18
  98.8 0.0 collective-permute-done.17.refs_5_
  98.8 0.0 collective-permute-done.19.refs_7_
  98.8 0.0 collective-permute-done.14.refs_2_
  98.8 1.9 %collective-permute-done.16.refs_4_ = f32[2,4,256]{2,1,0:T(4,128)S(1)} collective-permute-done((f32[2,4,256]{2,1,0:T(4,128)S(1)}, f32[2,4,256]{2,1,0:T(4,128)S(1)}, u32[]{:S(2)}, u32[]{:S(2)}) %collective-permute-start.16) | collective-permute-done | bytes 8224 | tf_op jit(solution)/shard_map/ppermute | solution.py:457
  100.7 1.1 %collective-permute-done.18.refs_6_ = f32[2,4,256]{2,1,0:T(4,128)S(1)} collective-permute-done((f32[2,4,256]{2,1,0:T(4,128)S(1)}, f32[2,4,256]{2,1,0:T(4,128)S(1)}, u32[]{:S(2)}, u32[]{:S(2)}) %collective-permute-start.18) | collective-permute-done | bytes 8224 | tf_op jit(solution)/shard_map/ppermute | solution.py:457
  101.7 0.6 join_columns.1
Async XLA Ops:
  7.3 2.5 %collective-permute-start.4 = (bf16[1,50,2,16,256]{4,3,2,1,0:T(8,128)(2,1)S(1)}, bf16[1,50,2,16,256]{4,3,2,1,0:T(8,128)(2,1)S(1)}, u32[]{:S(2)}, u32[]{:S(2)}) collective-permute-start(bf16[1,50,2,16,256]{4,3,2,1,0:T(8,128)(2,1)S(1)} %get-tuple-element.38.refs_8_), channel_id=1, source_target_pairs={{0,8},{8,0},{16,24},{24,16},{1,9},{9,1},{17,25},{25,17},{2,10},{10... | collective-permute-start | bytes 2457608 | tf_op jit(solution)/shard_map/ppermute | solution.py:457
  15.0 2.4 %collective-permute-start.5 = (bf16[1,50,2,16,256]{4,3,2,1,0:T(8,128)(2,1)S(1)}, bf16[1,50,2,16,256]{4,3,2,1,0:T(8,128)(2,1)S(1)}, u32[]{:S(2)}, u32[]{:S(2)}) collective-permute-start(bf16[1,50,2,16,256]{4,3,2,1,0:T(8,128)(2,1)S(1)} %get-tuple-element.42.refs_7_), channel_id=1, source_target_pairs={{0,8},{8,0},{16,24},{24,16},{1,9},{9,1},{17,25},{25,17},{2,10},{10... | collective-permute-start | bytes 2457608 | tf_op jit(solution)/shard_map/ppermute | solution.py:457
  24.2 49.2 %collective-permute-start.6 = (bf16[2,50,2,16,256]{4,3,2,1,0:T(8,128)(2,1)S(1)}, bf16[2,50,2,16,256]{4,3,2,1,0:T(8,128)(2,1)S(1)}, u32[]{:S(2)}, u32[]{:S(2)}) collective-permute-start(bf16[2,50,2,16,256]{4,3,2,1,0:T(8,128)(2,1)S(1)} %local_terms.8.refs_7_), channel_id=1, source_target_pairs={{0,8},{8,0},{16,24},{24,16},{1,9},{9,1},{17,25},{25,17},{2,10},{10... | collective-permute-start | bytes 4915208 | tf_op jit(solution)/shard_map/ppermute | solution.py:457
  24.6 12.2 %collective-permute-start.11 = (bf16[6,3,2,16,256]{4,3,2,1,0:T(8,128)(2,1)S(1)}, bf16[6,3,2,16,256]{4,3,2,1,0:T(8,128)(2,1)S(1)}, u32[]{:S(2)}, u32[]{:S(2)}) collective-permute-start(bf16[6,3,2,16,256]{4,3,2,1,0:T(8,128)(2,1)S(1)} %get-tuple-element.45.refs_3_), channel_id=1, source_target_pairs={{1,3},{2,0},{3,5},{4,2},{5,7},{6,4},{9,11},{10,8},{11,13},{12,10},... | collective-permute-start | bytes 884744 | tf_op jit(solution)/shard_map/ppermute | solution.py:460
  25.9 22.8 %collective-permute-start = (bf16[8,3,2,16,256]{4,3,2,1,0:T(8,128)(2,1)S(1)}, bf16[8,3,2,16,256]{4,3,2,1,0:T(8,128)(2,1)S(1)}, u32[]{:S(2)}, u32[]{:S(2)}) collective-permute-start(bf16[8,3,2,16,256]{4,3,2,1,0:T(8,128)(2,1)S(1)} %get-tuple-element.29.rest_4_.refs_0_), channel_id=1, source_target_pairs={{0,1},{1,0},{2,3},{3,2},{4,5},{5,4},{6,7},{7,6},{8,9},{9,8},{10,11... | collective-permute-start | bytes 1179656 | tf_op jit(solution)/shard_map/ppermute | solution.py:460
  30.8 16.3 %collective-permute-start.10 = (bf16[6,3,2,16,256]{4,3,2,1,0:T(8,128)(2,1)S(1)}, bf16[6,3,2,16,256]{4,3,2,1,0:T(8,128)(2,1)S(1)}, u32[]{:S(2)}, u32[]{:S(2)}) collective-permute-start(bf16[6,3,2,16,256]{4,3,2,1,0:T(8,128)(2,1)S(1)} %get-tuple-element.45.refs_3_), channel_id=1, source_target_pairs={{0,1},{1,0},{2,3},{3,2},{4,5},{5,4},{6,7},{7,6},{8,9},{9,8},{10,11... | collective-permute-start | bytes 884744 | tf_op jit(solution)/shard_map/ppermute | solution.py:460
  30.9 24.6 %collective-permute-start.2 = (bf16[8,3,2,16,256]{4,3,2,1,0:T(8,128)(2,1)S(1)}, bf16[8,3,2,16,256]{4,3,2,1,0:T(8,128)(2,1)S(1)}, u32[]{:S(2)}, u32[]{:S(2)}) collective-permute-start(bf16[8,3,2,16,256]{4,3,2,1,0:T(8,128)(2,1)S(1)} %get-tuple-element.30.refs_3_), channel_id=1, source_target_pairs={{0,1},{1,0},{2,3},{3,2},{4,5},{5,4},{6,7},{7,6},{8,9},{9,8},{10,11... | collective-permute-start | bytes 1179656 | tf_op jit(solution)/shard_map/ppermute | solution.py:460
  36.8 29.3 %collective-permute-start.8 = (bf16[10,3,2,16,256]{4,3,2,1,0:T(8,128)(2,1)S(1)}, bf16[10,3,2,16,256]{4,3,2,1,0:T(8,128)(2,1)S(1)}, u32[]{:S(2)}, u32[]{:S(2)}) collective-permute-start(bf16[10,3,2,16,256]{4,3,2,1,0:T(8,128)(2,1)S(1)} %get-tuple-element.44.refs_0_), channel_id=1, source_target_pairs={{0,1},{1,0},{2,3},{3,2},{4,5},{5,4},{6,7},{7,6},{8,9},{9,8},{10,11... | collective-permute-start | bytes 1474568 | tf_op jit(solution)/shard_map/ppermute | solution.py:460
  47.1 34.1 %collective-permute-start.13 = (bf16[1,50,2,16,256]{4,3,2,1,0:T(8,128)(2,1)S(1)}, bf16[1,50,2,16,256]{4,3,2,1,0:T(8,128)(2,1)S(1)}, u32[]{:S(2)}, u32[]{:S(2)}) collective-permute-start(bf16[1,50,2,16,256]{4,3,2,1,0:T(8,128)(2,1)S(1)} %local_terms.7.refs_7_), channel_id=1, source_target_pairs={{0,16},{8,24},{16,0},{24,8},{1,17},{9,25},{17,1},{25,9},{2,18},{10... | collective-permute-start | bytes 2457608 | tf_op jit(solution)/shard_map/ppermute | solution.py:457
  48.7 47.3 %collective-permute-start.7 = (bf16[1,50,2,16,256]{4,3,2,1,0:T(8,128)(2,1)S(1)}, bf16[1,50,2,16,256]{4,3,2,1,0:T(8,128)(2,1)S(1)}, u32[]{:S(2)}, u32[]{:S(2)}) collective-permute-start(bf16[1,50,2,16,256]{4,3,2,1,0:T(8,128)(2,1)S(1)} %get-tuple-element.40.refs_8_), channel_id=1, source_target_pairs={{0,16},{8,24},{16,0},{24,8},{1,17},{9,25},{17,1},{25,9},{2,18},{10... | collective-permute-start | bytes 2457608 | tf_op jit(solution)/shard_map/ppermute | solution.py:457
  55.5 16.3 %collective-permute-start.12 = (bf16[6,3,2,16,256]{4,3,2,1,0:T(8,128)(2,1)S(1)}, bf16[6,3,2,16,256]{4,3,2,1,0:T(8,128)(2,1)S(1)}, u32[]{:S(2)}, u32[]{:S(2)}) collective-permute-start(bf16[6,3,2,16,256]{4,3,2,1,0:T(8,128)(2,1)S(1)} %collective-permute-done.11), channel_id=1, source_target_pairs={{0,1},{1,0},{2,3},{3,2},{4,5},{5,4},{6,7},{7,6},{8,9},{9,8},{10,11... | collective-permute-start | bytes 884744 | tf_op jit(solution)/shard_map/ppermute | solution.py:460
  66.0 15.1 %collective-permute-start.9 = (bf16[10,3,2,16,256]{4,3,2,1,0:T(8,128)(2,1)S(1)}, bf16[10,3,2,16,256]{4,3,2,1,0:T(8,128)(2,1)S(1)}, u32[]{:S(2)}, u32[]{:S(2)}) collective-permute-start(bf16[10,3,2,16,256]{4,3,2,1,0:T(8,128)(2,1)S(1)} %collective-permute-done.8.refs_1_), channel_id=1, source_target_pairs={{0,2},{2,4},{3,1},{4,6},{5,3},{7,5},{8,10},{10,12},{11,9},{12,14},... | collective-permute-start | bytes 1474568 | tf_op jit(solution)/shard_map/ppermute | solution.py:460
  71.8 17.8 %collective-permute-start.1 = (bf16[8,3,2,16,256]{4,3,2,1,0:T(8,128)(2,1)S(1)}, bf16[8,3,2,16,256]{4,3,2,1,0:T(8,128)(2,1)S(1)}, u32[]{:S(2)}, u32[]{:S(2)}) collective-permute-start(bf16[8,3,2,16,256]{4,3,2,1,0:T(8,128)(2,1)S(1)} %collective-permute-done.refs_1_), channel_id=1, source_target_pairs={{0,2},{1,7},{2,4},{3,1},{4,6},{5,3},{6,0},{7,5},{8,10},{9,15},{10,... | collective-permute-start | bytes 1179656 | tf_op jit(solution)/shard_map/ppermute | solution.py:460
  73.4 22.6 %collective-permute-start.3 = (bf16[8,3,2,16,256]{4,3,2,1,0:T(8,128)(2,1)S(1)}, bf16[8,3,2,16,256]{4,3,2,1,0:T(8,128)(2,1)S(1)}, u32[]{:S(2)}, u32[]{:S(2)}) collective-permute-start(bf16[8,3,2,16,256]{4,3,2,1,0:T(8,128)(2,1)S(1)} %collective-permute-done.2.refs_4_), channel_id=1, source_target_pairs={{0,2},{1,7},{2,4},{3,1},{4,6},{5,3},{6,0},{7,5},{8,10},{9,15},{10,... | collective-permute-start | bytes 1179656 | tf_op jit(solution)/shard_map/ppermute | solution.py:460
  82.1 16.6 %collective-permute-start.15 = (f32[2,4,256]{2,1,0:T(4,128)S(1)}, f32[2,4,256]{2,1,0:T(4,128)S(1)}, u32[]{:S(2)}, u32[]{:S(2)}) collective-permute-start(f32[2,4,256]{2,1,0:T(4,128)S(1)} %get-tuple-element.48), channel_id=1, source_target_pairs={{0,8},{8,0},{16,24},{24,16},{1,9},{9,1},{17,25},{25,17},{2,10},{10... | collective-permute-start | bytes 24584 | tf_op jit(solution)/shard_map/ppermute | solution.py:457
  82.2 16.7 %collective-permute-start.17 = (f32[2,4,256]{2,1,0:T(4,128)S(1)}, f32[2,4,256]{2,1,0:T(4,128)S(1)}, u32[]{:S(2)}, u32[]{:S(2)}) collective-permute-start(f32[2,4,256]{2,1,0:T(4,128)S(1)} %get-tuple-element.50), channel_id=1, source_target_pairs={{0,16},{8,24},{16,0},{24,8},{1,17},{9,25},{17,1},{25,9},{2,18},{10... | collective-permute-start | bytes 24584 | tf_op jit(solution)/shard_map/ppermute | solution.py:457
  89.6 9.2 %collective-permute-start.19 = (f32[2,4,256]{2,1,0:T(4,128)S(1)}, f32[2,4,256]{2,1,0:T(4,128)S(1)}, u32[]{:S(2)}, u32[]{:S(2)}) collective-permute-start(f32[2,4,256]{2,1,0:T(4,128)S(1)} %get-tuple-element.52), channel_id=1, source_target_pairs={{0,24},{8,16},{16,8},{24,0},{1,25},{9,17},{17,9},{25,1},{2,26},{10... | collective-permute-start | bytes 24584 | tf_op jit(solution)/shard_map/ppermute | solution.py:457
  96.9 1.9 %collective-permute-start.14 = (f32[2,4,256]{2,1,0:T(4,128)S(1)}, f32[2,4,256]{2,1,0:T(4,128)S(1)}, u32[]{:S(2)}, u32[]{:S(2)}) collective-permute-start(f32[2,4,256]{2,1,0:T(4,128)S(1)} %get-tuple-element.47), channel_id=1, source_target_pairs={{0,8},{8,0},{16,24},{24,16},{1,9},{9,1},{17,25},{25,17},{2,10},{10... | collective-permute-start | bytes 24584 | tf_op jit(solution)/shard_map/ppermute | solution.py:457
  97.0 3.7 %collective-permute-start.16 = (f32[2,4,256]{2,1,0:T(4,128)S(1)}, f32[2,4,256]{2,1,0:T(4,128)S(1)}, u32[]{:S(2)}, u32[]{:S(2)}) collective-permute-start(f32[2,4,256]{2,1,0:T(4,128)S(1)} %get-tuple-element.49), channel_id=1, source_target_pairs={{0,16},{8,24},{16,0},{24,8},{1,17},{9,25},{17,1},{25,9},{2,18},{10... | collective-permute-start | bytes 24584 | tf_op jit(solution)/shard_map/ppermute | solution.py:457
  98.6 3.1 %collective-permute-start.18 = (f32[2,4,256]{2,1,0:T(4,128)S(1)}, f32[2,4,256]{2,1,0:T(4,128)S(1)}, u32[]{:S(2)}, u32[]{:S(2)}) collective-permute-start(f32[2,4,256]{2,1,0:T(4,128)S(1)} %get-tuple-element.51), channel_id=1, source_target_pairs={{0,24},{8,16},{16,8},{24,0},{1,25},{9,17},{17,9},{25,1},{2,26},{10... | collective-permute-start | bytes 24584 | tf_op jit(solution)/shard_map/ppermute | solution.py:457
where the time goes:
time: 103 us; the launch traced here: 102 us
  waiting for transfers between devices  51.2 us (50%)
  Pallas kernels  26.4 us (26%)
  starting transfers between devices  24.6 us (24%)
    ppermute x9, waiting for transfers between devices, along(): return lax.ppermute(x, 'slab', links)  44.3 us
    ppermute x9, starting transfers between devices, along(): return lax.ppermute(x, 'slab', links)  17.6 us
    pallas_call x5, Pallas kernels, local_terms(): pl.pallas_call(functools.partial(local_kernel, bits=bits, first=first, wa...  16.7 us
    ppermute x11, starting transfers between devices, swap(): return lax.ppermute(x, 'rcv', [(i, i ^ bit) for i in range(groups)])  6.99 us
    ppermute x11, waiting for transfers between devices, swap(): return lax.ppermute(x, 'rcv', [(i, i ^ bit) for i in range(groups)])  6.85 us
    pallas_call x1, Pallas kernels, first_terms(): pl.pallas_call(functools.partial(first_kernel, bits=bits, waits=len(after...  5.92 us
  transfers between devices with their start and end apart: 20, of which 12 were waited for; matrix products, arithmetic and copies ran while one was open for 0% of the time, Pallas kernels for 6%

commit v1 on v0

--- a/solution.py
+++ b/solution.py
@@ -233,9 +233,9 @@
     return ref.at[..., pl.ds(pl.multiple_of(half * 2 * width, 2 * width), 2 * width)]
 
 
-def first_kernel(me_ref, filters_ref, pairs_ref, u_src, green_src, *rest, bits, waits):
+def first_kernel(me_ref, filters_src, pairs_src, u_src, green_src, *rest, bits, waits):
     (lam_src, mu_src, dcol_src, drow_src), rest = rest[:4], rest[4 + waits :]
-    z_ref, green_ref, mix_ref, dcol_ref, drow_ref, u_ref, lam_ref, mu_ref, gs, xs, ys, sems = rest
+    z_ref, green_ref, mix_ref, dcol_ref, drow_ref, u_ref, lam_ref, mu_ref, gs, xs, ys, filters_ref, pairs_ref, sems = rest
     rows, width = z_ref.shape[-2:]
     me = me_ref[0]
     block = me ^ bits
@@ -251,6 +251,12 @@
     late = [green_block(block ^ 1, sems.at[5])]
     for copy in early:
         copy.start()
+    scalars = ((filters_src, filters_ref), (pairs_src, pairs_ref))
+    scalars = [pltpu.make_async_copy(src, ref, sems.at[7 + k]) for k, (src, ref) in enumerate(scalars)]
+    for copy in scalars:
+        copy.start()
+    for copy in scalars:
+        copy.wait()
     fill_mix(filters_ref, pairs_ref, mix_ref, rows // 2)
     for copy in early:
         copy.wait()
@@ -297,9 +303,11 @@
     z, near, *tables = pl.pallas_call(
         functools.partial(first_kernel, bits=bits, waits=len(after)),
         out_shape=[z_shape(1, displacement, width)] + [pltpu.VMEM(*one) for one in kept],
-        in_specs=[SMEM] * 3 + [ANY] * (6 + len(after)),
+        in_specs=[SMEM] + [ANY] * (8 + len(after)),
         out_specs=[VMEM] * (1 + len(kept)),
-        scratch_shapes=local_scratch(displacement, width) + [pltpu.SemaphoreType.DMA((7,))],
+        scratch_shapes=local_scratch(displacement, width)
+        + [pltpu.SMEM(array.shape, array.dtype) for array in (filters, pairs)]
+        + [pltpu.SemaphoreType.DMA((9,))],
         cost_estimate=local_cost(1, green, displacement, width),
         compiler_params=pltpu.CompilerParams(vmem_limit_bytes=16 * 2**20),
         name="first_terms",

time: 103 us -> 102 us (level)
  no operation moved by 1% of the time
where the time goes in v1:
time: 102 us
  waiting for transfers between devices  51.1 us (50%)
  Pallas kernels  25.7 us (25%)
  starting transfers between devices  24.6 us (24%)
    ppermute x9, waiting for transfers between devices, along(): return lax.ppermute(x, 'slab', links)  44.4 us
    ppermute x9, starting transfers between devices, along(): return lax.ppermute(x, 'slab', links)  17.6 us
    pallas_call x5, Pallas kernels, local_terms(): pl.pallas_call(functools.partial(local_kernel, bits=bits, first=first, wa...  16.7 us
    ppermute x11, starting transfers between devices, swap(): return lax.ppermute(x, 'rcv', [(i, i ^ bit) for i in range(groups)])  6.99 us
    ppermute x11, waiting for transfers between devices, swap(): return lax.ppermute(x, 'rcv', [(i, i ^ bit) for i in range(groups)])  6.72 us
    pallas_call x1, Pallas kernels, first_terms(): pl.pallas_call(functools.partial(first_kernel, bits=bits, waits=len(after...  5.18 us
  transfers between devices with their start and end apart: 20, of which 12 were waited for; matrix products, arithmetic and copies ran while one was open for 0% of the time, Pallas kernels for 6%

profile of v1, /device:TPU:0, one launch (start us, length us, event | category | flops | bytes accessed | tf_op | source)
XLA Modules:
  0.0 101.5 jit_solution(4057962774139783207)
XLA Ops:
  0.0 1.4 %own_columns.1 = (bf16[8,3,2,16,256]{4,3,2,1,0:T(8,128)(2,1)S(1)}, bf16[8,3,2,16,256]{4,3,2,1,0:T(8,128)(2,1)S(1)}, bf16[10,3,2,16,256]{4,3,2,1,0:T(8,128)(2,1)S(1)}, bf16[6,3,2,16,256]{4,3,2,1,0:T(8,128)(2,1)S(1)}) custom-call(s32[1]{0:T(128)} %bitcast.me_ref, s32[1]{0:T(128)} %bitcast.1.slab_ref, bf16[2,16,3,2,16,1024]{5,4,3,2,1,0:T(8,128)(2,1)} %refs_7_.2), custom_call_target="tpu_custom_call" | custom-call | tf_op jit(solution)/shard_map/own_columns/pallas_call | solution.py:107
  1.4 5.2 %first_terms.1 = (bf16[1,50,2,16,256]{4,3,2,1,0:T(8,128)(2,1)S(1)}, bf16[2,16,6,2,16,512]{5,4,3,2,1,0:T(8,128)(2,1)S(1)}, bf16[256,512]{1,0:T(8,128)(2,1)S(1)}, ...) custom-call(s32[1]{0:T(128)} %bitcast.me_ref, ...), custom_call_target="tpu_custom_call" | custom-call | flops 1207959552 | bytes 5505024 | tf_op jit(solution)/shard_map/first_terms/pallas_call | solution.py:303
  6.6 0.5 collective-permute-start.4
  7.1 2.0 %collective-permute-done.4.refs_9_ = bf16[1,50,2,16,256]{4,3,2,1,0:T(8,128)(2,1)S(1)} collective-permute-done((bf16[1,50,2,16,256]{4,3,2,1,0:T(8,128)(2,1)S(1)}, bf16[1,50,2,16,256]{4,3,2,1,0:T(8,128)(2,1)S(1)}, u32[]{:S(2)}, u32[]{:S(2)}) %collective-permute-start.4) | collective-permute-done | bytes 819232 | tf_op jit(solution)/shard_map/ppermute | solution.py:465
  9.1 2.3 %local_terms.5 = (bf16[1,50,2,16,256]{4,3,2,1,0:T(8,128)(2,1)S(1)}, bf16[2,16,3,2,16,1024]{5,4,3,2,1,0:T(8,128)(2,1)S(1)}) custom-call(s32[1]{0:T(128)} %bitcast.me_ref, bf16[256,512]{1,0:T(8,128)(2,1)S(1)} %get-tuple-element.31.refs_0_, bf16[256,256]{1,0:T(8,128)(2,1)S(1)} %get-tuple-element.32.refs_1_, ...), custom_call_target="tpu_custom_call", output_to_operand_aliasing={{1}: (4, {})} | custom-call | flops 1207959552 | bytes 5505024 | tf_op jit(solution)/shard_map/local_terms/pallas_call | solution.py:351
  11.4 2.8 %local_terms.6 = (bf16[1,50,2,16,256]{4,3,2,1,0:T(8,128)(2,1)S(1)}, bf16[2,16,6,2,16,512]{5,4,3,2,1,0:T(8,128)(2,1)S(1)}) custom-call(s32[1]{0:T(128)} %bitcast.me_ref, bf16[256,512]{1,0:T(8,128)(2,1)S(1)} %get-tuple-element.31.refs_0_, bf16[256,256]{1,0:T(8,128)(2,1)S(1)} %get-tuple-element.32.refs_1_, bf16[2,128,256]{2,1,0:T(8,128)(2,1)S(1)} %get-tuple-element.33.refs_2_, ...), custom_call_target="tpu_custom_call" | custom-call | flops 1207959552 | bytes 5505024 | tf_op jit(solution)/shard_map/local_terms/pallas_call | solution.py:351
  14.2 0.4 collective-permute-start.5
  14.7 2.0 %collective-permute-done.5.refs_8_ = bf16[1,50,2,16,256]{4,3,2,1,0:T(8,128)(2,1)S(1)} collective-permute-done((bf16[1,50,2,16,256]{4,3,2,1,0:T(8,128)(2,1)S(1)}, bf16[1,50,2,16,256]{4,3,2,1,0:T(8,128)(2,1)S(1)}, u32[]{:S(2)}, u32[]{:S(2)}) %collective-permute-start.5) | collective-permute-done | bytes 819232 | tf_op jit(solution)/shard_map/ppermute | solution.py:465
  16.6 2.3 %local_terms.7.refs_7_ = bf16[1,50,2,16,256]{4,3,2,1,0:T(8,128)(2,1)S(1)} custom-call(s32[1]{0:T(128)} %bitcast.me_ref, bf16[256,512]{1,0:T(8,128)(2,1)S(1)} %get-tuple-element.31.refs_0_, bf16[256,256]{1,0:T(8,128)(2,1)S(1)} %get-tuple-element.32.refs_1_, bf16[2,128,256]{2,1,0:T(8,128)(2,1)S(1)} %get-tuple-element.33.refs_2_, ...), custom_call_target="tpu_custom_call" | custom-call | flops 1207959552 | bytes 5505024 | tf_op jit(solution)/shard_map/local_terms/pallas_call | solution.py:351
  19.0 4.5 %local_terms.8.refs_7_ = bf16[2,50,2,16,256]{4,3,2,1,0:T(8,128)(2,1)S(1)} custom-call(s32[1]{0:T(128)} %bitcast.me_ref, bf16[256,512]{1,0:T(8,128)(2,1)S(1)} %get-tuple-element.31.refs_0_, bf16[256,256]{1,0:T(8,128)(2,1)S(1)} %get-tuple-element.32.refs_1_, bf16[2,128,256]{2,1,0:T(8,128)(2,1)S(1)} %get-tuple-element.33.refs_2_, ...), custom_call_target="tpu_custom_call" | custom-call | flops 2415919104 | bytes 11010048 | tf_op jit(solution)/shard_map/local_terms/pallas_call | solution.py:351
  23.5 0.4 collective-permute-start.6
  23.9 1.3 %collective-permute-start.11 = (bf16[6,3,2,16,256]{4,3,2,1,0:T(8,128)(2,1)S(1)}, bf16[6,3,2,16,256]{4,3,2,1,0:T(8,128)(2,1)S(1)}, u32[]{:S(2)}, u32[]{:S(2)}) collective-permute-start(bf16[6,3,2,16,256]{4,3,2,1,0:T(8,128)(2,1)S(1)} %get-tuple-element.45.refs_3_), channel_id=1, source_target_pairs={{1,3},{2,0},{3,5},{4,2},{5,7},{6,4},{9,11},{10,8},{11,13},{12,10},... | collective-permute-start | bytes 884744 | tf_op jit(solution)/shard_map/ppermute | solution.py:468
  25.2 4.9 %collective-permute-start = (bf16[8,3,2,16,256]{4,3,2,1,0:T(8,128)(2,1)S(1)}, bf16[8,3,2,16,256]{4,3,2,1,0:T(8,128)(2,1)S(1)}, u32[]{:S(2)}, u32[]{:S(2)}) collective-permute-start(bf16[8,3,2,16,256]{4,3,2,1,0:T(8,128)(2,1)S(1)} %get-tuple-element.29.rest_4_.refs_0_), channel_id=1, source_target_pairs={{0,1},{1,0},{2,3},{3,2},{4,5},{5,4},{6,7},{7,6},{8,9},{9,8},{10,11... | collective-permute-start | bytes 1179656 | tf_op jit(solution)/shard_map/ppermute | solution.py:468
  30.1 0.1 collective-permute-start.10
  30.1 1.9 %collective-permute-start.2 = (bf16[8,3,2,16,256]{4,3,2,1,0:T(8,128)(2,1)S(1)}, bf16[8,3,2,16,256]{4,3,2,1,0:T(8,128)(2,1)S(1)}, u32[]{:S(2)}, u32[]{:S(2)}) collective-permute-start(bf16[8,3,2,16,256]{4,3,2,1,0:T(8,128)(2,1)S(1)} %get-tuple-element.30.refs_3_), channel_id=1, source_target_pairs={{0,1},{1,0},{2,3},{3,2},{4,5},{5,4},{6,7},{7,6},{8,9},{9,8},{10,11... | collective-permute-start | bytes 1179656 | tf_op jit(solution)/shard_map/ppermute | solution.py:468
  32.1 4.0 %collective-permute-done.11 = bf16[6,3,2,16,256]{4,3,2,1,0:T(8,128)(2,1)S(1)} collective-permute-done((bf16[6,3,2,16,256]{4,3,2,1,0:T(8,128)(2,1)S(1)}, bf16[6,3,2,16,256]{4,3,2,1,0:T(8,128)(2,1)S(1)}, u32[]{:S(2)}, u32[]{:S(2)}) %collective-permute-start.11) | collective-permute-done | bytes 294944 | tf_op jit(solution)/shard_map/ppermute | solution.py:468
  36.1 0.7 collective-permute-start.8
  36.8 9.6 %collective-permute-done.10.refs_4_ = bf16[6,3,2,16,256]{4,3,2,1,0:T(8,128)(2,1)S(1)} collective-permute-done((bf16[6,3,2,16,256]{4,3,2,1,0:T(8,128)(2,1)S(1)}, bf16[6,3,2,16,256]{4,3,2,1,0:T(8,128)(2,1)S(1)}, u32[]{:S(2)}, u32[]{:S(2)}) %collective-permute-start.10) | collective-permute-done | bytes 294944 | tf_op jit(solution)/shard_map/ppermute | solution.py:468
  46.4 1.6 %collective-permute-start.13 = (bf16[1,50,2,16,256]{4,3,2,1,0:T(8,128)(2,1)S(1)}, bf16[1,50,2,16,256]{4,3,2,1,0:T(8,128)(2,1)S(1)}, u32[]{:S(2)}, u32[]{:S(2)}) collective-permute-start(bf16[1,50,2,16,256]{4,3,2,1,0:T(8,128)(2,1)S(1)} %local_terms.7.refs_7_), channel_id=1, source_target_pairs={{0,16},{8,24},{16,0},{24,8},{1,17},{9,25},{17,1},{25,9},{2,18},{10... | collective-permute-start | bytes 2457608 | tf_op jit(solution)/shard_map/ppermute | solution.py:465
  47.9 0.0 collective-permute-done.refs_1_
  47.9 0.5 collective-permute-start.7
  48.4 6.4 %collective-permute-done.2.refs_4_ = bf16[8,3,2,16,256]{4,3,2,1,0:T(8,128)(2,1)S(1)} collective-permute-done((bf16[8,3,2,16,256]{4,3,2,1,0:T(8,128)(2,1)S(1)}, bf16[8,3,2,16,256]{4,3,2,1,0:T(8,128)(2,1)S(1)}, u32[]{:S(2)}, u32[]{:S(2)}) %collective-permute-start.2) | collective-permute-done | bytes 393248 | tf_op jit(solution)/shard_map/ppermute | solution.py:468
  54.8 2.0 %collective-permute-start.12 = (bf16[6,3,2,16,256]{4,3,2,1,0:T(8,128)(2,1)S(1)}, bf16[6,3,2,16,256]{4,3,2,1,0:T(8,128)(2,1)S(1)}, u32[]{:S(2)}, u32[]{:S(2)}) collective-permute-start(bf16[6,3,2,16,256]{4,3,2,1,0:T(8,128)(2,1)S(1)} %collective-permute-done.11), channel_id=1, source_target_pairs={{0,1},{1,0},{2,3},{3,2},{4,5},{5,4},{6,7},{7,6},{8,9},{9,8},{10,11... | collective-permute-start | bytes 884744 | tf_op jit(solution)/shard_map/ppermute | solution.py:468
  56.8 8.5 %collective-permute-done.8.refs_1_ = bf16[10,3,2,16,256]{4,3,2,1,0:T(8,128)(2,1)S(1)} collective-permute-done((bf16[10,3,2,16,256]{4,3,2,1,0:T(8,128)(2,1)S(1)}, bf16[10,3,2,16,256]{4,3,2,1,0:T(8,128)(2,1)S(1)}, u32[]{:S(2)}, u32[]{:S(2)}) %collective-permute-start.8) | collective-permute-done | bytes 491552 | tf_op jit(solution)/shard_map/ppermute | solution.py:468
  65.3 3.5 %collective-permute-start.9 = (bf16[10,3,2,16,256]{4,3,2,1,0:T(8,128)(2,1)S(1)}, bf16[10,3,2,16,256]{4,3,2,1,0:T(8,128)(2,1)S(1)}, u32[]{:S(2)}, u32[]{:S(2)}) collective-permute-start(bf16[10,3,2,16,256]{4,3,2,1,0:T(8,128)(2,1)S(1)} %collective-permute-done.8.refs_1_), channel_id=1, source_target_pairs={{0,2},{2,4},{3,1},{4,6},{5,3},{7,5},{8,10},{10,12},{11,9},{12,14},... | collective-permute-start | bytes 1474568 | tf_op jit(solution)/shard_map/ppermute | solution.py:468
  68.8 2.3 %collective-permute-done.12.refs_5_ = bf16[6,3,2,16,256]{4,3,2,1,0:T(8,128)(2,1)S(1)} collective-permute-done((bf16[6,3,2,16,256]{4,3,2,1,0:T(8,128)(2,1)S(1)}, bf16[6,3,2,16,256]{4,3,2,1,0:T(8,128)(2,1)S(1)}, u32[]{:S(2)}, u32[]{:S(2)}) %collective-permute-start.12) | collective-permute-done | bytes 294944 | tf_op jit(solution)/shard_map/ppermute | solution.py:468
  71.1 1.6 %collective-permute-start.1 = (bf16[8,3,2,16,256]{4,3,2,1,0:T(8,128)(2,1)S(1)}, bf16[8,3,2,16,256]{4,3,2,1,0:T(8,128)(2,1)S(1)}, u32[]{:S(2)}, u32[]{:S(2)}) collective-permute-start(bf16[8,3,2,16,256]{4,3,2,1,0:T(8,128)(2,1)S(1)} %collective-permute-done.refs_1_), channel_id=1, source_target_pairs={{0,2},{1,7},{2,4},{3,1},{4,6},{5,3},{6,0},{7,5},{8,10},{9,15},{10,... | collective-permute-start | bytes 1179656 | tf_op jit(solution)/shard_map/ppermute | solution.py:468
  72.6 0.0 collective-permute-done.6.refs_8_
  72.6 1.6 %collective-permute-start.3 = (bf16[8,3,2,16,256]{4,3,2,1,0:T(8,128)(2,1)S(1)}, bf16[8,3,2,16,256]{4,3,2,1,0:T(8,128)(2,1)S(1)}, u32[]{:S(2)}, u32[]{:S(2)}) collective-permute-start(bf16[8,3,2,16,256]{4,3,2,1,0:T(8,128)(2,1)S(1)} %collective-permute-done.2.refs_4_), channel_id=1, source_target_pairs={{0,2},{1,7},{2,4},{3,1},{4,6},{5,3},{6,0},{7,5},{8,10},{9,15},{10,... | collective-permute-start | bytes 1179656 | tf_op jit(solution)/shard_map/ppermute | solution.py:468
  74.2 4.7 %local_terms.9.refs_6_ = bf16[2,50,2,16,256]{4,3,2,1,0:T(8,128)(2,1)S(1)} custom-call(s32[1]{0:T(128)} %bitcast.me_ref, bf16[256,512]{1,0:T(8,128)(2,1)S(1)} %get-tuple-element.31.refs_0_, bf16[256,256]{1,0:T(8,128)(2,1)S(1)} %get-tuple-element.32.refs_1_, bf16[2,128,256]{2,1,0:T(8,128)(2,1)S(1)} %get-tuple-element.33.refs_2_, ...), custom_call_target="tpu_custom_call" | custom-call | flops 2415919104 | bytes 11010048 | tf_op jit(solution)/shard_map/local_terms/pallas_call | solution.py:351
  78.9 1.4 %collective-permute-done.9.refs_2_ = bf16[10,3,2,16,256]{4,3,2,1,0:T(8,128)(2,1)S(1)} collective-permute-done((bf16[10,3,2,16,256]{4,3,2,1,0:T(8,128)(2,1)S(1)}, bf16[10,3,2,16,256]{4,3,2,1,0:T(8,128)(2,1)S(1)}, u32[]{:S(2)}, u32[]{:S(2)}) %collective-permute-start.9) | collective-permute-done | bytes 491552 | tf_op jit(solution)/shard_map/ppermute | solution.py:468
  80.4 0.0 collective-permute-done.13.refs_7_
  80.4 0.9 depth_terms.3
  81.3 0.1 collective-permute-start.15
  81.4 1.6 %collective-permute-start.17 = (f32[2,4,256]{2,1,0:T(4,128)S(1)}, f32[2,4,256]{2,1,0:T(4,128)S(1)}, u32[]{:S(2)}, u32[]{:S(2)}) collective-permute-start(f32[2,4,256]{2,1,0:T(4,128)S(1)} %get-tuple-element.50), channel_id=1, source_target_pairs={{0,16},{8,24},{16,0},{24,8},{1,17},{9,25},{17,1},{25,9},{2,18},{10... | collective-permute-start | bytes 24584 | tf_op jit(solution)/shard_map/ppermute | solution.py:465
  83.0 5.8 %collective-permute-done.1.refs_2_ = bf16[8,3,2,16,256]{4,3,2,1,0:T(8,128)(2,1)S(1)} collective-permute-done((bf16[8,3,2,16,256]{4,3,2,1,0:T(8,128)(2,1)S(1)}, bf16[8,3,2,16,256]{4,3,2,1,0:T(8,128)(2,1)S(1)}, u32[]{:S(2)}, u32[]{:S(2)}) %collective-permute-start.1) | collective-permute-done | bytes 393248 | tf_op jit(solution)/shard_map/ppermute | solution.py:468
  88.8 0.0 collective-permute-start.19
  88.8 6.4 %collective-permute-done.3.refs_5_ = bf16[8,3,2,16,256]{4,3,2,1,0:T(8,128)(2,1)S(1)} collective-permute-done((bf16[8,3,2,16,256]{4,3,2,1,0:T(8,128)(2,1)S(1)}, bf16[8,3,2,16,256]{4,3,2,1,0:T(8,128)(2,1)S(1)}, u32[]{:S(2)}, u32[]{:S(2)}) %collective-permute-start.3) | collective-permute-done | bytes 393248 | tf_op jit(solution)/shard_map/ppermute | solution.py:468
  95.2 0.0 collective-permute-done.7.refs_7_
  95.2 0.9 depth_terms.2
  96.2 0.1 collective-permute-start.14
  96.2 1.6 %collective-permute-start.16 = (f32[2,4,256]{2,1,0:T(4,128)S(1)}, f32[2,4,256]{2,1,0:T(4,128)S(1)}, u32[]{:S(2)}, u32[]{:S(2)}) collective-permute-start(f32[2,4,256]{2,1,0:T(4,128)S(1)} %get-tuple-element.49), channel_id=1, source_target_pairs={{0,16},{8,24},{16,0},{24,8},{1,17},{9,25},{17,1},{25,9},{2,18},{10... | collective-permute-start | bytes 24584 | tf_op jit(solution)/shard_map/ppermute | solution.py:465
  97.8 0.0 collective-permute-done.15.refs_3_
  97.8 0.3 collective-permute-start.18
  98.1 0.0 collective-permute-done.17.refs_5_
  98.1 0.0 collective-permute-done.19.refs_7_
  98.1 0.0 collective-permute-done.14.refs_2_
  98.1 1.9 %collective-permute-done.16.refs_4_ = f32[2,4,256]{2,1,0:T(4,128)S(1)} collective-permute-done((f32[2,4,256]{2,1,0:T(4,128)S(1)}, f32[2,4,256]{2,1,0:T(4,128)S(1)}, u32[]{:S(2)}, u32[]{:S(2)}) %collective-permute-start.16) | collective-permute-done | bytes 8224 | tf_op jit(solution)/shard_map/ppermute | solution.py:465
  100.0 0.9 collective-permute-done.18.refs_6_
  100.9 0.6 join_columns.1
Async XLA Ops:
  6.6 2.5 %collective-permute-start.4 = (bf16[1,50,2,16,256]{4,3,2,1,0:T(8,128)(2,1)S(1)}, bf16[1,50,2,16,256]{4,3,2,1,0:T(8,128)(2,1)S(1)}, u32[]{:S(2)}, u32[]{:S(2)}) collective-permute-start(bf16[1,50,2,16,256]{4,3,2,1,0:T(8,128)(2,1)S(1)} %get-tuple-element.38.refs_8_), channel_id=1, source_target_pairs={{0,8},{8,0},{16,24},{24,16},{1,9},{9,1},{17,25},{25,17},{2,10},{10... | collective-permute-start | bytes 2457608 | tf_op jit(solution)/shard_map/ppermute | solution.py:465
  14.2 2.4 %collective-permute-start.5 = (bf16[1,50,2,16,256]{4,3,2,1,0:T(8,128)(2,1)S(1)}, bf16[1,50,2,16,256]{4,3,2,1,0:T(8,128)(2,1)S(1)}, u32[]{:S(2)}, u32[]{:S(2)}) collective-permute-start(bf16[1,50,2,16,256]{4,3,2,1,0:T(8,128)(2,1)S(1)} %get-tuple-element.42.refs_7_), channel_id=1, source_target_pairs={{0,8},{8,0},{16,24},{24,16},{1,9},{9,1},{17,25},{25,17},{2,10},{10... | collective-permute-start | bytes 2457608 | tf_op jit(solution)/shard_map/ppermute | solution.py:465
  23.5 49.2 %collective-permute-start.6 = (bf16[2,50,2,16,256]{4,3,2,1,0:T(8,128)(2,1)S(1)}, bf16[2,50,2,16,256]{4,3,2,1,0:T(8,128)(2,1)S(1)}, u32[]{:S(2)}, u32[]{:S(2)}) collective-permute-start(bf16[2,50,2,16,256]{4,3,2,1,0:T(8,128)(2,1)S(1)} %local_terms.8.refs_7_), channel_id=1, source_target_pairs={{0,8},{8,0},{16,24},{24,16},{1,9},{9,1},{17,25},{25,17},{2,10},{10... | collective-permute-start | bytes 4915208 | tf_op jit(solution)/shard_map/ppermute | solution.py:465
  23.9 12.2 %collective-permute-start.11 = (bf16[6,3,2,16,256]{4,3,2,1,0:T(8,128)(2,1)S(1)}, bf16[6,3,2,16,256]{4,3,2,1,0:T(8,128)(2,1)S(1)}, u32[]{:S(2)}, u32[]{:S(2)}) collective-permute-start(bf16[6,3,2,16,256]{4,3,2,1,0:T(8,128)(2,1)S(1)} %get-tuple-element.45.refs_3_), channel_id=1, source_target_pairs={{1,3},{2,0},{3,5},{4,2},{5,7},{6,4},{9,11},{10,8},{11,13},{12,10},... | collective-permute-start | bytes 884744 | tf_op jit(solution)/shard_map/ppermute | solution.py:468
  25.2 22.8 %collective-permute-start = (bf16[8,3,2,16,256]{4,3,2,1,0:T(8,128)(2,1)S(1)}, bf16[8,3,2,16,256]{4,3,2,1,0:T(8,128)(2,1)S(1)}, u32[]{:S(2)}, u32[]{:S(2)}) collective-permute-start(bf16[8,3,2,16,256]{4,3,2,1,0:T(8,128)(2,1)S(1)} %get-tuple-element.29.rest_4_.refs_0_), channel_id=1, source_target_pairs={{0,1},{1,0},{2,3},{3,2},{4,5},{5,4},{6,7},{7,6},{8,9},{9,8},{10,11... | collective-permute-start | bytes 1179656 | tf_op jit(solution)/shard_map/ppermute | solution.py:468
  30.1 16.3 %collective-permute-start.10 = (bf16[6,3,2,16,256]{4,3,2,1,0:T(8,128)(2,1)S(1)}, bf16[6,3,2,16,256]{4,3,2,1,0:T(8,128)(2,1)S(1)}, u32[]{:S(2)}, u32[]{:S(2)}) collective-permute-start(bf16[6,3,2,16,256]{4,3,2,1,0:T(8,128)(2,1)S(1)} %get-tuple-element.45.refs_3_), channel_id=1, source_target_pairs={{0,1},{1,0},{2,3},{3,2},{4,5},{5,4},{6,7},{7,6},{8,9},{9,8},{10,11... | collective-permute-start | bytes 884744 | tf_op jit(solution)/shard_map/ppermute | solution.py:468
  30.1 24.6 %collective-permute-start.2 = (bf16[8,3,2,16,256]{4,3,2,1,0:T(8,128)(2,1)S(1)}, bf16[8,3,2,16,256]{4,3,2,1,0:T(8,128)(2,1)S(1)}, u32[]{:S(2)}, u32[]{:S(2)}) collective-permute-start(bf16[8,3,2,16,256]{4,3,2,1,0:T(8,128)(2,1)S(1)} %get-tuple-element.30.refs_3_), channel_id=1, source_target_pairs={{0,1},{1,0},{2,3},{3,2},{4,5},{5,4},{6,7},{7,6},{8,9},{9,8},{10,11... | collective-permute-start | bytes 1179656 | tf_op jit(solution)/shard_map/ppermute | solution.py:468
  36.1 29.2 %collective-permute-start.8 = (bf16[10,3,2,16,256]{4,3,2,1,0:T(8,128)(2,1)S(1)}, bf16[10,3,2,16,256]{4,3,2,1,0:T(8,128)(2,1)S(1)}, u32[]{:S(2)}, u32[]{:S(2)}) collective-permute-start(bf16[10,3,2,16,256]{4,3,2,1,0:T(8,128)(2,1)S(1)} %get-tuple-element.44.refs_0_), channel_id=1, source_target_pairs={{0,1},{1,0},{2,3},{3,2},{4,5},{5,4},{6,7},{7,6},{8,9},{9,8},{10,11... | collective-permute-start | bytes 1474568 | tf_op jit(solution)/shard_map/ppermute | solution.py:468
  46.4 34.0 %collective-permute-start.13 = (bf16[1,50,2,16,256]{4,3,2,1,0:T(8,128)(2,1)S(1)}, bf16[1,50,2,16,256]{4,3,2,1,0:T(8,128)(2,1)S(1)}, u32[]{:S(2)}, u32[]{:S(2)}) collective-permute-start(bf16[1,50,2,16,256]{4,3,2,1,0:T(8,128)(2,1)S(1)} %local_terms.7.refs_7_), channel_id=1, source_target_pairs={{0,16},{8,24},{16,0},{24,8},{1,17},{9,25},{17,1},{25,9},{2,18},{10... | collective-permute-start | bytes 2457608 | tf_op jit(solution)/shard_map/ppermute | solution.py:465
  47.9 47.3 %collective-permute-start.7 = (bf16[1,50,2,16,256]{4,3,2,1,0:T(8,128)(2,1)S(1)}, bf16[1,50,2,16,256]{4,3,2,1,0:T(8,128)(2,1)S(1)}, u32[]{:S(2)}, u32[]{:S(2)}) collective-permute-start(bf16[1,50,2,16,256]{4,3,2,1,0:T(8,128)(2,1)S(1)} %get-tuple-element.40.refs_8_), channel_id=1, source_target_pairs={{0,16},{8,24},{16,0},{24,8},{1,17},{9,25},{17,1},{25,9},{2,18},{10... | collective-permute-start | bytes 2457608 | tf_op jit(solution)/shard_map/ppermute | solution.py:465
  54.8 16.3 %collective-permute-start.12 = (bf16[6,3,2,16,256]{4,3,2,1,0:T(8,128)(2,1)S(1)}, bf16[6,3,2,16,256]{4,3,2,1,0:T(8,128)(2,1)S(1)}, u32[]{:S(2)}, u32[]{:S(2)}) collective-permute-start(bf16[6,3,2,16,256]{4,3,2,1,0:T(8,128)(2,1)S(1)} %collective-permute-done.11), channel_id=1, source_target_pairs={{0,1},{1,0},{2,3},{3,2},{4,5},{5,4},{6,7},{7,6},{8,9},{9,8},{10,11... | collective-permute-start | bytes 884744 | tf_op jit(solution)/shard_map/ppermute | solution.py:468
  65.3 15.1 %collective-permute-start.9 = (bf16[10,3,2,16,256]{4,3,2,1,0:T(8,128)(2,1)S(1)}, bf16[10,3,2,16,256]{4,3,2,1,0:T(8,128)(2,1)S(1)}, u32[]{:S(2)}, u32[]{:S(2)}) collective-permute-start(bf16[10,3,2,16,256]{4,3,2,1,0:T(8,128)(2,1)S(1)} %collective-permute-done.8.refs_1_), channel_id=1, source_target_pairs={{0,2},{2,4},{3,1},{4,6},{5,3},{7,5},{8,10},{10,12},{11,9},{12,14},... | collective-permute-start | bytes 1474568 | tf_op jit(solution)/shard_map/ppermute | solution.py:468
  71.1 17.7 %collective-permute-start.1 = (bf16[8,3,2,16,256]{4,3,2,1,0:T(8,128)(2,1)S(1)}, bf16[8,3,2,16,256]{4,3,2,1,0:T(8,128)(2,1)S(1)}, u32[]{:S(2)}, u32[]{:S(2)}) collective-permute-start(bf16[8,3,2,16,256]{4,3,2,1,0:T(8,128)(2,1)S(1)} %collective-permute-done.refs_1_), channel_id=1, source_target_pairs={{0,2},{1,7},{2,4},{3,1},{4,6},{5,3},{6,0},{7,5},{8,10},{9,15},{10,... | collective-permute-start | bytes 1179656 | tf_op jit(solution)/shard_map/ppermute | solution.py:468
  72.6 22.6 %collective-permute-start.3 = (bf16[8,3,2,16,256]{4,3,2,1,0:T(8,128)(2,1)S(1)}, bf16[8,3,2,16,256]{4,3,2,1,0:T(8,128)(2,1)S(1)}, u32[]{:S(2)}, u32[]{:S(2)}) collective-permute-start(bf16[8,3,2,16,256]{4,3,2,1,0:T(8,128)(2,1)S(1)} %collective-permute-done.2.refs_4_), channel_id=1, source_target_pairs={{0,2},{1,7},{2,4},{3,1},{4,6},{5,3},{6,0},{7,5},{8,10},{9,15},{10,... | collective-permute-start | bytes 1179656 | tf_op jit(solution)/shard_map/ppermute | solution.py:468
  81.3 16.5 %collective-permute-start.15 = (f32[2,4,256]{2,1,0:T(4,128)S(1)}, f32[2,4,256]{2,1,0:T(4,128)S(1)}, u32[]{:S(2)}, u32[]{:S(2)}) collective-permute-start(f32[2,4,256]{2,1,0:T(4,128)S(1)} %get-tuple-element.48), channel_id=1, source_target_pairs={{0,8},{8,0},{16,24},{24,16},{1,9},{9,1},{17,25},{25,17},{2,10},{10... | collective-permute-start | bytes 24584 | tf_op jit(solution)/shard_map/ppermute | solution.py:465
  81.4 16.7 %collective-permute-start.17 = (f32[2,4,256]{2,1,0:T(4,128)S(1)}, f32[2,4,256]{2,1,0:T(4,128)S(1)}, u32[]{:S(2)}, u32[]{:S(2)}) collective-permute-start(f32[2,4,256]{2,1,0:T(4,128)S(1)} %get-tuple-element.50), channel_id=1, source_target_pairs={{0,16},{8,24},{16,0},{24,8},{1,17},{9,25},{17,1},{25,9},{2,18},{10... | collective-permute-start | bytes 24584 | tf_op jit(solution)/shard_map/ppermute | solution.py:465
  88.8 9.3 %collective-permute-start.19 = (f32[2,4,256]{2,1,0:T(4,128)S(1)}, f32[2,4,256]{2,1,0:T(4,128)S(1)}, u32[]{:S(2)}, u32[]{:S(2)}) collective-permute-start(f32[2,4,256]{2,1,0:T(4,128)S(1)} %get-tuple-element.52), channel_id=1, source_target_pairs={{0,24},{8,16},{16,8},{24,0},{1,25},{9,17},{17,9},{25,1},{2,26},{10... | collective-permute-start | bytes 24584 | tf_op jit(solution)/shard_map/ppermute | solution.py:465
  96.2 1.9 %collective-permute-start.14 = (f32[2,4,256]{2,1,0:T(4,128)S(1)}, f32[2,4,256]{2,1,0:T(4,128)S(1)}, u32[]{:S(2)}, u32[]{:S(2)}) collective-permute-start(f32[2,4,256]{2,1,0:T(4,128)S(1)} %get-tuple-element.47), channel_id=1, source_target_pairs={{0,8},{8,0},{16,24},{24,16},{1,9},{9,1},{17,25},{25,17},{2,10},{10... | collective-permute-start | bytes 24584 | tf_op jit(solution)/shard_map/ppermute | solution.py:465
  96.2 3.7 %collective-permute-start.16 = (f32[2,4,256]{2,1,0:T(4,128)S(1)}, f32[2,4,256]{2,1,0:T(4,128)S(1)}, u32[]{:S(2)}, u32[]{:S(2)}) collective-permute-start(f32[2,4,256]{2,1,0:T(4,128)S(1)} %get-tuple-element.49), channel_id=1, source_target_pairs={{0,16},{8,24},{16,0},{24,8},{1,17},{9,25},{17,1},{25,9},{2,18},{10... | collective-permute-start | bytes 24584 | tf_op jit(solution)/shard_map/ppermute | solution.py:465
  97.8 3.1 %collective-permute-start.18 = (f32[2,4,256]{2,1,0:T(4,128)S(1)}, f32[2,4,256]{2,1,0:T(4,128)S(1)}, u32[]{:S(2)}, u32[]{:S(2)}) collective-permute-start(f32[2,4,256]{2,1,0:T(4,128)S(1)} %get-tuple-element.51), channel_id=1, source_target_pairs={{0,24},{8,16},{16,8},{24,0},{1,25},{9,17},{17,9},{25,1},{2,26},{10... | collective-permute-start | bytes 24584 | tf_op jit(solution)/shard_map/ppermute | solution.py:465
